TPU v7x, 256 devices: a whole 4x4x8 slice. The times are simulated.
256 devices in a mesh: seq: 32 (over z, y), chan: 8 (over x, core).
Axes of the slice: x: 4, y: 4, z: 8, core: 2. Of those that a mesh axis runs over, the one named last changes fastest.
Arguments:
- hyena_query: bfloat16 [4096, 8192], P('chan', 'seq'), may hold values from -36 to 36
- hyena_key: bfloat16 [4096, 8192], P('chan', 'seq'), may hold values from -6 to 6
- hyena_value: bfloat16 [4096, 8192], P('chan', 'seq'), may hold values from -6 to 6
- long_filter: float32 [4096, 8192], P(('chan', 'seq')), may hold values from -4 to 4
- skip_weight: float32 [4096], P(('chan', 'seq')), may hold values from 0.5 to 1.5
- stripe_order: int32 [8192], replicated, may hold values from 0 to 8191, as said below
- query_rows: bfloat16 [8192, 4096], P('seq', 'chan'), may hold values from -6 to 6
- key_rows: bfloat16 [8192, 4096], P('seq', 'chan'), may hold values from -6 to 6
- norm_gain: float32 [4096], P('chan'), may hold values from 0.1 to 1.9
Outputs:
- hyena_output: bfloat16 [4096, 8192], P('chan', 'seq')
- attended: bfloat16 [8192, 4096], P('seq', 'chan')
Inputs may be any that keep to these rules, and one draw needn't show every extreme that they name: stripe_order[256 * s + j] = 32 * j + sigma(s) for 0 <= j < 256 and 0 <= s < 32, where sigma is a permutation of 0 to 31.
All inputs are finite; a program needn't handle non-finite values.
Results may differ from a plain program's by a relative error of at most 0.012.
Values may be sent and summed in bfloat16 or wider, within the bound.
No kernel may reach another device: no remote copies, remote signals or barrier semaphores. Data moves between devices by JAX's collectives and lax.ppermute only.
A program may use at most 128 MiB of HBM per device.

v0:
```python
import math
import jax
import jax.numpy as jnp
from jax import lax
from jax.sharding import PartitionSpec as P

D = 4096
HEAD_DIM = 128


def angle_table(first, second, modulus):
    left = jnp.arange(first, dtype=jnp.int32)[:, None]
    right = jnp.arange(second, dtype=jnp.int32)[None, :]
    theta = 2.0 * math.pi / modulus * (left * right % modulus).astype(jnp.float32)
    return (jnp.cos(theta), jnp.sin(theta))


def transform_tables(length):
    outer = 2 * length // 128
    first_cos, first_sin = angle_table(outer, outer // 2, outer)
    twist_cos, twist_sin = angle_table(outer, 128, 2 * length)
    inner_cos, inner_sin = angle_table(128, 128, 128)
    return (first_cos, first_sin, twist_cos, twist_sin, inner_cos, inner_sin)


def contract(form, left, right):
    return jnp.einsum(form, left, right, precision=lax.Precision.HIGHEST)


def forward(signal, tables):
    first_cos, first_sin, twist_cos, twist_sin, inner_cos, inner_sin = tables
    section_real = contract("kt,cts->cks", first_cos, signal)
    section_imag = -contract("kt,cts->cks", first_sin, signal)
    turned_real = section_real * twist_cos + section_imag * twist_sin
    turned_imag = section_imag * twist_cos - section_real * twist_sin
    out_real = contract("cks,sm->ckm", turned_real, inner_cos) + contract(
        "cks,sm->ckm", turned_imag, inner_sin
    )
    out_imag = contract("cks,sm->ckm", turned_imag, inner_cos) - contract(
        "cks,sm->ckm", turned_real, inner_sin
    )
    return (out_real, out_imag)


def inverse(spectrum_real, spectrum_imag, tables):
    first_cos, first_sin, twist_cos, twist_sin, inner_cos, inner_sin = tables
    back_real = contract("ckm,sm->cks", spectrum_real, inner_cos) - contract(
        "ckm,sm->cks", spectrum_imag, inner_sin
    )
    back_imag = contract("ckm,sm->cks", spectrum_real, inner_sin) + contract(
        "ckm,sm->cks", spectrum_imag, inner_cos
    )
    turned_real = back_real * twist_cos - back_imag * twist_sin
    turned_imag = back_real * twist_sin + back_imag * twist_cos
    signal = contract("kt,cks->cts", first_cos, turned_real) - contract(
        "kt,cks->cts", first_sin, turned_imag
    )
    return signal * (1.0 / (first_cos.shape[0] * 128))


def convolve(signal, filter_parts, tables):
    pencil, length = signal.shape
    widened = signal.astype(jnp.float32).reshape(pencil, length // 128, 128)
    signal_real, signal_imag = forward(widened, tables)
    filter_real, filter_imag = filter_parts
    product_real = signal_real * filter_real - signal_imag * filter_imag
    product_imag = signal_real * filter_imag + signal_imag * filter_real
    return inverse(product_real, product_imag, tables).reshape(pencil, length)


def fold_keys(carry, queries, own_places, key_piece, value_piece, places, scale):
    count = key_piece.shape[0]
    heads = queries.shape[1]
    depth = queries.shape[2]
    block = math.gcd(count, 512)
    place_blocks = places.reshape(count // block, block)
    key_blocks = key_piece.reshape(count // block, block, heads, depth)
    value_blocks = value_piece.reshape(count // block, block, heads, depth)

    def one_block(state, inputs):
        running, totals, sums = state
        key_block, value_block, key_places = inputs
        scores = (
            jnp.einsum("qhd,khd->hqk", queries, key_block, preferred_element_type=jnp.float32)
            * scale
        )
        allowed = key_places[None, None, :] <= own_places[None, :, None]
        scores = jnp.where(allowed, scores, -1e30)
        highest = jnp.maximum(running, jnp.max(scores, axis=2))
        weights = jnp.where(allowed, jnp.exp(scores - highest[:, :, None]), 0.0)
        factor = jnp.exp(running - highest)
        totals = totals * factor + jnp.sum(weights, axis=2)
        update = jnp.einsum(
            "hqk,khd->hqd",
            weights.astype(jnp.bfloat16),
            value_block,
            preferred_element_type=jnp.float32,
        )
        sums = sums * factor[:, :, None] + update
        return ((highest, totals, sums), None)

    carry, unused = lax.scan(one_block, carry, (key_blocks, value_blocks, place_blocks))
    return carry


def local(
    hyena_query,
    hyena_key,
    hyena_value,
    long_filter,
    skip_weight,
    stripe_order,
    query_rows,
    key_rows,
    norm_gain,
):
    stripes = lax.axis_size("seq")
    channels, rows = hyena_query.shape
    pencil, length = long_filter.shape
    sigma = stripe_order.reshape(stripes, rows)[:, 0]
    product = (hyena_key.astype(jnp.float32) * hyena_value.astype(jnp.float32)).astype(jnp.bfloat16)
    tables = transform_tables(length)
    filter_parts = forward(long_filter.reshape(pencil, length // 128, 128), tables)
    spread = lax.all_to_all(product, "seq", split_axis=0, concat_axis=1, tiled=True)
    summed = convolve(spread, filter_parts, tables) + skip_weight[:, None] * spread.astype(
        jnp.float32
    )
    returned = lax.all_to_all(
        summed.astype(jnp.bfloat16), "seq", split_axis=1, concat_axis=0, tiled=True
    ).astype(summed.dtype)
    gated = (hyena_query.astype(jnp.float32) * returned).astype(jnp.bfloat16)
    per_stripe = rows // stripes
    columns = stripes * jnp.arange(per_stripe, dtype=jnp.int32)[None, :] + sigma[:, None]
    arranged = jnp.take(gated, columns.reshape(rows), axis=1).reshape(channels, stripes, per_stripe)
    banded = lax.all_to_all(arranged, "seq", split_axis=1, concat_axis=2, tiled=True).reshape(
        channels, rows
    )
    output_wide = banded.astype(jnp.float32)
    squares = lax.psum(jnp.sum(output_wide * output_wide, axis=0), "chan")
    inverse_rms = lax.rsqrt(squares / D + 1e-05)
    normed = (output_wide * inverse_rms[None, :] * norm_gain[:, None]).astype(jnp.bfloat16)
    value_rows = normed.T
    local_heads = channels // HEAD_DIM
    scale = 1.0 / math.sqrt(HEAD_DIM)
    seq_index = lax.axis_index("seq")
    own_places = lax.dynamic_slice_in_dim(stripe_order, seq_index * rows, rows)
    queries = query_rows.reshape(rows, local_heads, HEAD_DIM)
    initial = (
        jnp.full((local_heads, rows), -1e30, jnp.float32),
        jnp.zeros((local_heads, rows), jnp.float32),
        jnp.zeros((local_heads, rows, HEAD_DIM), jnp.float32),
    )
    key_piece = lax.all_gather(key_rows, "seq", axis=0, tiled=True)
    value_piece = lax.all_gather(value_rows, "seq", axis=0, tiled=True)
    running, totals, sums = fold_keys(
        initial, queries, own_places, key_piece, value_piece, stripe_order, scale
    )
    attended = (
        (sums / totals[:, :, None]).transpose(1, 0, 2).reshape(rows, channels).astype(jnp.bfloat16)
    )
    return (banded, attended)


def solution(mesh):
    placed = (
        P("chan", "seq"),
        P("chan", "seq"),
        P("chan", "seq"),
        P(("chan", "seq"), None),
        P(("chan", "seq")),
        P(),
        P("seq", "chan"),
        P("seq", "chan"),
        P("chan"),
    )
    return jax.shard_map(
        local,
        mesh=mesh,
        in_specs=placed,
        out_specs=(P("chan", "seq"), P("seq", "chan")),
        check_vma=False,
    )
```

profile of v0, /device:TPU:1, one launch (start us, length us, event | category | flops | bytes accessed | tf_op | source)
XLA Modules:
  0.0 309.6 jit_solution(8558879919215344293)
XLA Ops:
  7.9 1.8 multiply_convert_fusion.2
  9.7 12.0 %all-to-all-start = ((bf16[32,16,256]{2,1,0:T(8,128)(2,1)}), bf16[32,16,256]{2,1,0:T(8,128)(2,1)S(1)}, u32[]{:S(2)}, u32[]{:S(2)}) async-start(bf16[32,16,256]{2,1,0:T(8,128)(2,1)} %bitcast), calls=%async_computation | async-start | bytes 524288 | tf_op jit(solution)/shard_map/all_to_all | solution.py:124
  30.1 2.9 all-to-all-done
  34.7 2.0 fusion.34
  36.8 2.2 fusion.35
  39.0 2.0 convolution_add_fusion.3
  41.0 2.2 multiply_add_fusion
  50.0 1.7 fusion.15
  52.9 6.3 %all-to-all-start.1 = ((bf16[16,32,256]{2,0,1:T(8,128)(2,1)}), bf16[16,32,256]{2,0,1:T(8,128)(2,1)S(1)}, u32[]{:S(2)}, u32[]{:S(2)}) async-start(bf16[16,32,256]{2,0,1:T(8,128)(2,1)} %fusion.29), calls=%async_computation.1 | async-start | bytes 524288 | tf_op jit(solution)/shard_map/all_to_all | solution.py:128
  59.4 10.5 %all-to-all-done.1 = bf16[16,32,256]{2,0,1:T(8,128)(2,1)S(1)} async-done(((bf16[16,32,256]{2,0,1:T(8,128)(2,1)}), bf16[16,32,256]{2,0,1:T(8,128)(2,1)S(1)}, u32[]{:S(2)}, u32[]{:S(2)}) %all-to-all-start.1) | async-done | bytes 262176 | tf_op jit(solution)/shard_map/all_to_all | solution.py:128
  71.5 17.9 %all_to_all.35 = bf16[512,32,8]{0,2,1:T(8,128)(2,1)S(1)} all-to-all(bf16[512,32,8]{0,2,1:T(8,128)(2,1)S(1)} %bitcast_select_fusion.1), channel_id=1, replica_groups=mesh['seq'=32,'chan'=8] {'seq'}, dimensions={1} | all-to-all | bytes 524288 | tf_op jit(solution)/shard_map/all_to_all | solution.py:135
  89.6 16.4 %psum.7 = f32[256]{0:T(256)S(1)} all-reduce(f32[256]{0:T(256)S(1)} %reduce_sum.21), channel_id=1, replica_groups=mesh['seq'=32,'chan'=8] {'chan'}, use_global_device_ids=true, to_apply=%region_1.2 | all-reduce | flops 256 | bytes 2048 | tf_op jit(solution)/shard_map/psum | solution.py:139
  108.8 6.7 %all-gather.3.cloned.1.call-done = bf16[8192,512]{1,0:T(8,128)(2,1)} async-done(((bf16[256,512]{1,0:T(8,128)(2,1)}), bf16[8192,512]{1,0:T(8,128)(2,1)}) %all-gather.3.cloned.1.call-update) | async-done | bytes 8388624 | tf_op jit(solution)/shard_map/all_gather | solution.py:153
  115.6 12.6 %reshape.201 = bf16[16,512,4,128]{3,2,1,0:T(4,128)(2,1)} reshape(bf16[8192,512]{1,0:T(8,128)(2,1)} %all-gather.3.cloned.1.call-done) | data formatting | bytes 16777216 | tf_op jit(solution)/shard_map/reshape | solution.py:77
  128.1 86.4 %all-gather.5.cloned.1.call-done = bf16[8192,512]{1,0:T(8,128)(2,1)} async-done(((bf16[256,512]{1,0:T(8,128)(2,1)}), bf16[8192,512]{1,0:T(8,128)(2,1)}) %all-gather.5.cloned.1.call-update) | async-done | bytes 8388624 | tf_op jit(solution)/shard_map/all_gather | solution.py:154
  214.5 12.5 %reshape.187 = bf16[16,512,4,128]{3,2,1,0:T(4,128)(2,1)} reshape(bf16[8192,512]{1,0:T(8,128)(2,1)} %all-gather.5.cloned.1.call-done) | data formatting | bytes 16777216 | tf_op jit(solution)/shard_map/reshape | solution.py:78
  227.0 74.9 %while.15 = (s32[]{:T(128)}, f32[4,256]{1,0:T(4,128)S(1)}, f32[4,256]{1,0:T(4,128)S(1)}, f32[4,256,128]{2,1,0:T(8,128)S(1)}, s32[16,512]{1,0:T(8,128)}, /*index=...) while((s32[]{:T(128)}, f32[4,256]{1,0:T(4,128)S(1)}, ...), condition=%wide.region_5.6_spmd.clone, body=%wide.region_2.5_spmd.clone.sunk | while | flops 275780608 | bytes 11345025 | solution.py:102
  227.9 1.6 constant_dynamic-slice_fusion.6
  232.6 1.6 constant_dynamic-slice_fusion.6
  237.2 1.6 constant_dynamic-slice_fusion.6
  241.9 1.6 constant_dynamic-slice_fusion.6
  246.6 1.6 constant_dynamic-slice_fusion.6
  251.3 1.6 constant_dynamic-slice_fusion.6
  256.0 1.6 constant_dynamic-slice_fusion.6
  260.6 1.6 constant_dynamic-slice_fusion.6
  265.3 1.6 constant_dynamic-slice_fusion.6
  270.0 1.6 constant_dynamic-slice_fusion.6
  274.7 1.6 constant_dynamic-slice_fusion.6
  279.4 1.6 constant_dynamic-slice_fusion.6
  284.1 1.6 constant_dynamic-slice_fusion.6
  293.4 1.6 constant_dynamic-slice_fusion.6
  298.1 1.6 constant_dynamic-slice_fusion.6
  (193 shorter events, 74.6 us)
Async XLA Ops:
  7.2 15.1 %copy-start = (f32[16,8192]{1,0:T(8,128)S(1)}, f32[16,8192]{1,0:T(8,128)}, u32[]{:S(2)}) copy-start(f32[16,8192]{1,0:T(8,128)} %param.14) | copy-start | bytes 1572868
  7.2 15.2 %copy-start.1 = (bf16[512,256]{1,0:T(8,128)(2,1)S(1)}, bf16[512,256]{1,0:T(8,128)(2,1)}, u32[]{:S(2)}) copy-start(bf16[512,256]{1,0:T(8,128)(2,1)} %param.11) | copy-start | bytes 786436
  7.2 15.3 %copy-start.3 = (s32[8192]{0:T(1024)S(1)}, s32[8192]{0:T(1024)}, u32[]{:S(2)}) copy-start(s32[8192]{0:T(1024)} %param.16) | copy-start | bytes 98308
  7.2 108.4 %all-gather.3.cloned.1.call-start = ((), (), s32[]{:S(2)}) async-start(), calls=%async_computation.3 | async-start | bytes 8650752 | tf_op jit(solution)/shard_map/all_gather | solution.py:153
  9.7 23.3 %all-to-all-start = ((bf16[32,16,256]{2,1,0:T(8,128)(2,1)}), bf16[32,16,256]{2,1,0:T(8,128)(2,1)S(1)}, u32[]{:S(2)}, u32[]{:S(2)}) async-start(bf16[32,16,256]{2,1,0:T(8,128)(2,1)} %bitcast), calls=%async_computation | async-start | bytes 524288 | tf_op jit(solution)/shard_map/all_to_all | solution.py:124
  50.0 1.9 copy-start.5
  52.9 17.0 %all-to-all-start.1 = ((bf16[16,32,256]{2,0,1:T(8,128)(2,1)}), bf16[16,32,256]{2,0,1:T(8,128)(2,1)S(1)}, u32[]{:S(2)}, u32[]{:S(2)}) async-start(bf16[16,32,256]{2,0,1:T(8,128)(2,1)} %fusion.29), calls=%async_computation.1 | async-start | bytes 524288 | tf_op jit(solution)/shard_map/all_to_all | solution.py:128
  59.2 155.3 %all-gather.5.cloned.1.call-start = ((), (), s32[]{:S(2)}) async-start(), calls=%async_computation.4 | async-start | bytes 8650752 | tf_op jit(solution)/shard_map/all_gather | solution.py:154
  70.2 35.9 %copy-start.4 = (f32[512]{0:T(512)S(1)}, f32[512]{0:T(512)}, u32[]{:S(2)}) copy-start(f32[512]{0:T(512)} %param.19) | copy-start | bytes 6148
  70.2 37.4 %copy-start.2 = (bf16[256,512]{1,0:T(8,128)(2,1)S(1)}, bf16[256,512]{1,0:T(8,128)(2,1)}, u32[]{:S(2)}) copy-start(bf16[256,512]{1,0:T(8,128)(2,1)} %param.17) | copy-start | bytes 786436
Sparse Core Ops, SparseCore 0:
  10.6 104.9 all-gather.2
  118.7 95.7 all-gather.4
where the time goes:
time: 312 us; the launch traced here: 310 us
  waiting for transfers between devices  107 us (34%)
  local copies, waits for them, and re-layouts  66.1 us (21%)
  matrix products  51.7 us (17%)
  blocking collectives  34.4 us (11%)
  starting transfers between devices  18.4 us (6%)
  other arithmetic  16.6 us (5%)
  between operations  14.4 us (5%)
    all_gather x1, waiting for transfers between devices, local(): value_piece = lax.all_gather(value_rows, 'seq', axis=0, tiled=True)  86.4 us
    dynamic_slice x32, local copies, waits for them, and re-layouts, fold_keys(): lax.scan(one_block, carry, (key_blocks, value_blocks, place_blocks))  36.7 us
    dot_general x18, matrix products, contract(): return jnp.einsum(form, left, right, precision=lax.Precision.HIGHEST)  25.7 us
    all_to_all x1, blocking collectives, local(): lax.all_to_all(arranged, 'seq', split_axis=1, concat_axis=2, tiled=True)  17.9 us
    dot_general x16, matrix products, one_block(): jnp.einsum('hqk,khd->hqd', weights.astype(jnp.bfloat16), value_block, pre...  17.9 us
    psum x1, blocking collectives, local(): squares = lax.psum(jnp.sum(output_wide * output_wide, axis=0), 'chan')  16.4 us
    reshape x1, local copies, waits for them, and re-layouts, fold_keys(): key_blocks = key_piece.reshape(count // block, block, heads, depth)  12.6 us
    reshape x1, local copies, waits for them, and re-layouts, fold_keys(): value_blocks = value_piece.reshape(count // block, block, heads, depth)  12.5 us
  transfers between devices with their start and end apart: 4, of which 4 were waited for; matrix products, arithmetic and copies ran while one was open for 15% of the time, Pallas kernels for 0%

commit v1 on v0

--- a/solution.py
+++ b/solution.py
@@ -150,8 +150,11 @@
         jnp.zeros((local_heads, rows), jnp.float32),
         jnp.zeros((local_heads, rows, HEAD_DIM), jnp.float32),
     )
-    key_piece = lax.all_gather(key_rows, "seq", axis=0, tiled=True)
-    value_piece = lax.all_gather(value_rows, "seq", axis=0, tiled=True)
+    key_piece, value_piece = jnp.split(
+        lax.all_gather(jnp.concatenate([key_rows, value_rows], axis=1), "seq", axis=0, tiled=True),
+        [key_rows.shape[1]],
+        axis=1,
+    )
     running, totals, sums = fold_keys(
         initial, queries, own_places, key_piece, value_piece, stripe_order, scale
     )

time: 312 us -> 362 us (1.16)
  waiting for transfers between devices: 107 us -> 141 us
  local copies, waits for them, and re-layouts: 66.1 us -> 81.1 us
    all_gather x2 -> x1, waiting for transfers between devices: 93.1 us -> 130 us  [local(): lax.all_gather(jnp.concatenate([key_rows, value_rows], axis=1), 'seq', ax...]
    split x0 -> x1, local copies, waits for them, and re-layouts: none -> 11.3 us  [local(): jnp.split(lax.all_gather(jnp.concatenate([key_rows, value_rows], axis=1),...]
  transfers between devices with their start and end apart: 4 -> 3, of which waited for: 4 -> 2; matrix products, arithmetic and copies ran while one was open for 15% -> 4% of each run, Pallas kernels for 0% -> 0%
where the time goes in v1:
time: 362 us; the launch traced here: 359 us
  waiting for transfers between devices  141 us (39%)
  local copies, waits for them, and re-layouts  81.1 us (22%)
  matrix products  52.5 us (15%)
  blocking collectives  30.8 us (9%)
  starting transfers between devices  21.3 us (6%)
  other arithmetic  17.7 us (5%)
  between operations  14.4 us (4%)
    all_gather x1, waiting for transfers between devices, local(): lax.all_gather(jnp.concatenate([key_rows, value_rows], axis=1), 'seq', ax...  130 us
    dynamic_slice x32, local copies, waits for them, and re-layouts, fold_keys(): lax.scan(one_block, carry, (key_blocks, value_blocks, place_blocks))  36.7 us
    dot_general x18, matrix products, contract(): return jnp.einsum(form, left, right, precision=lax.Precision.HIGHEST)  26.5 us
    dot_general x16, matrix products, one_block(): jnp.einsum('hqk,khd->hqd', weights.astype(jnp.bfloat16), value_block, pre...  17.9 us
    psum x1, blocking collectives, local(): squares = lax.psum(jnp.sum(output_wide * output_wide, axis=0), 'chan')  15.5 us
    all_to_all x1, blocking collectives, local(): lax.all_to_all(arranged, 'seq', split_axis=1, concat_axis=2, tiled=True)  15.3 us
    reshape x1, local copies, waits for them, and re-layouts, fold_keys(): key_blocks = key_piece.reshape(count // block, block, heads, depth)  12.6 us
    reshape x1, local copies, waits for them, and re-layouts, fold_keys(): value_blocks = value_piece.reshape(count // block, block, heads, depth)  12.6 us
  transfers between devices with their start and end apart: 3, of which 2 were waited for; matrix products, arithmetic and copies ran while one was open for 4% of the time, Pallas kernels for 0%

profile of v1, /device:TPU:1, one launch (start us, length us, event | category | flops | bytes accessed | tf_op | source)
XLA Modules:
  0.0 359.5 jit_solution(1111706419539439511)
XLA Ops:
  7.2 1.8 multiply_convert_fusion.2
  9.0 12.2 %all-to-all-start = ((bf16[32,16,256]{2,1,0:T(8,128)(2,1)}), bf16[32,16,256]{2,1,0:T(8,128)(2,1)}, u32[]{:S(2)}, u32[]{:S(2)}) async-start(bf16[32,16,256]{2,1,0:T(8,128)(2,1)} %bitcast), calls=%async_computation | async-start | bytes 524288 | tf_op jit(solution)/shard_map/all_to_all | solution.py:124
  27.6 1.8 copy.56
  30.9 2.2 convolution_add_fusion.2
  35.8 2.0 fusion.34
  37.8 2.2 fusion.35
  40.0 2.0 convolution_add_fusion.3
  42.1 2.2 multiply_add_fusion
  50.9 1.7 fusion.15
  52.8 2.0 fusion.29
  54.8 9.1 %all-to-all-start.1 = ((bf16[16,32,256]{2,0,1:T(8,128)(2,1)}), bf16[16,32,256]{2,0,1:T(8,128)(2,1)S(1)}, u32[]{:S(2)}, u32[]{:S(2)}) async-start(bf16[16,32,256]{2,0,1:T(8,128)(2,1)} %fusion.29), calls=%async_computation.1 | async-start | bytes 524288 | tf_op jit(solution)/shard_map/all_to_all | solution.py:128
  64.1 10.5 %all-to-all-done.1 = bf16[16,32,256]{2,0,1:T(8,128)(2,1)S(1)} async-done(((bf16[16,32,256]{2,0,1:T(8,128)(2,1)}), bf16[16,32,256]{2,0,1:T(8,128)(2,1)S(1)}, u32[]{:S(2)}, u32[]{:S(2)}) %all-to-all-start.1) | async-done | bytes 262176 | tf_op jit(solution)/shard_map/all_to_all | solution.py:128
  76.2 15.3 %all_to_all.35 = bf16[512,32,8]{0,2,1:T(8,128)(2,1)S(1)} all-to-all(bf16[512,32,8]{0,2,1:T(8,128)(2,1)S(1)} %bitcast_select_fusion.1), channel_id=1, replica_groups=mesh['seq'=32,'chan'=8] {'seq'}, dimensions={1} | all-to-all | bytes 524288 | tf_op jit(solution)/shard_map/all_to_all | solution.py:135
  91.7 15.5 %psum.7 = f32[256]{0:T(256)S(1)} all-reduce(f32[256]{0:T(256)S(1)} %reduce_sum.21), channel_id=1, replica_groups=mesh['seq'=32,'chan'=8] {'chan'}, use_global_device_ids=true, to_apply=%region_1.2 | all-reduce | flops 256 | bytes 2048 | tf_op jit(solution)/shard_map/psum | solution.py:139
  110.2 130.2 %all-gather.2.cloned.1.call-done = bf16[8192,1024]{1,0:T(8,128)(2,1)} async-done(((bf16[256,1024]{1,0:T(8,128)(2,1)}), bf16[8192,1024]{1,0:T(8,128)(2,1)}) %all-gather.2.cloned.1.call-update) | async-done | bytes 16777232 | tf_op jit(solution)/shard_map/all_gather | solution.py:154
  240.4 11.3 %fusion.172 = (bf16[8192,512]{1,0:T(8,128)(2,1)}, bf16[8192,512]{1,0:T(8,128)(2,1)}) fusion(bf16[8192,1024]{1,0:T(8,128)(2,1)} %all-gather.2.cloned.1.call-done), kind=kLoop, calls=%fused_computation.209 | loop fusion | bytes 33554432 | tf_op jit(solution)/shard_map/split | solution.py:153
  251.7 12.6 %reshape.185 = bf16[16,512,4,128]{3,2,1,0:T(4,128)(2,1)} reshape(bf16[8192,512]{1,0:T(8,128)(2,1)} %get-tuple-element.138) | data formatting | bytes 16777216 | tf_op jit(solution)/shard_map/reshape | solution.py:77
  264.3 12.6 %reshape.187 = bf16[16,512,4,128]{3,2,1,0:T(4,128)(2,1)} reshape(bf16[8192,512]{1,0:T(8,128)(2,1)} %get-tuple-element.137) | data formatting | bytes 16777216 | tf_op jit(solution)/shard_map/reshape | solution.py:78
  276.8 74.9 %while.15 = (s32[]{:T(128)}, f32[4,256]{1,0:T(4,128)S(1)}, f32[4,256]{1,0:T(4,128)S(1)}, f32[4,256,128]{2,1,0:T(8,128)S(1)}, s32[16,512]{1,0:T(8,128)}, /*index=...) while((s32[]{:T(128)}, f32[4,256]{1,0:T(4,128)S(1)}, ...), condition=%wide.region_5.6_spmd.clone, body=%wide.region_2.5_spmd.clone.sunk | while | flops 275780608 | bytes 11345025 | solution.py:102
  277.7 1.6 constant_dynamic-slice_fusion.6
  282.4 1.6 constant_dynamic-slice_fusion.6
  287.0 1.6 constant_dynamic-slice_fusion.6
  291.7 1.6 constant_dynamic-slice_fusion.6
  301.1 1.6 constant_dynamic-slice_fusion.6
  305.8 1.6 constant_dynamic-slice_fusion.6
  310.5 1.6 constant_dynamic-slice_fusion.6
  319.8 1.6 constant_dynamic-slice_fusion.6
  324.5 1.6 constant_dynamic-slice_fusion.6
  329.2 1.6 constant_dynamic-slice_fusion.6
  338.6 1.6 constant_dynamic-slice_fusion.6
  343.2 1.6 constant_dynamic-slice_fusion.6
  347.9 1.6 constant_dynamic-slice_fusion.6
  (194 shorter events, 76.7 us)
Async XLA Ops:
  9.0 24.2 %all-to-all-start = ((bf16[32,16,256]{2,1,0:T(8,128)(2,1)}), bf16[32,16,256]{2,1,0:T(8,128)(2,1)}, u32[]{:S(2)}, u32[]{:S(2)}) async-start(bf16[32,16,256]{2,1,0:T(8,128)(2,1)} %bitcast), calls=%async_computation | async-start | bytes 524288 | tf_op jit(solution)/shard_map/all_to_all | solution.py:124
  26.3 3.1 copy-start.4
  40.0 2.1 copy-start
  50.9 1.9 copy-start.6
  52.6 22.2 %copy-start.1 = (bf16[512,256]{0,1:T(8,128)(2,1)S(1)}, bf16[512,256]{0,1:T(8,128)(2,1)}, u32[]{:S(2)}) copy-start(bf16[512,256]{0,1:T(8,128)(2,1)} %copy.56) | copy-start | bytes 786436
  54.8 19.8 %all-to-all-start.1 = ((bf16[16,32,256]{2,0,1:T(8,128)(2,1)}), bf16[16,32,256]{2,0,1:T(8,128)(2,1)S(1)}, u32[]{:S(2)}, u32[]{:S(2)}) async-start(bf16[16,32,256]{2,0,1:T(8,128)(2,1)} %fusion.29), calls=%async_computation.1 | async-start | bytes 524288 | tf_op jit(solution)/shard_map/all_to_all | solution.py:128
  63.9 176.5 %all-gather.2.cloned.1.call-start = ((), (), s32[]{:S(2)}) async-start(), calls=%async_computation.3 | async-start | bytes 17301504 | tf_op jit(solution)/shard_map/all_gather | solution.py:154
  74.9 32.4 %copy-start.5 = (f32[512]{0:T(512)S(1)}, f32[512]{0:T(512)}, u32[]{:S(2)}) copy-start(f32[512]{0:T(512)} %param.19) | copy-start | bytes 6148
  74.9 32.5 %copy-start.3 = (bf16[256,512]{1,0:T(8,128)(2,1)S(1)}, bf16[256,512]{1,0:T(8,128)(2,1)}, u32[]{:S(2)}) copy-start(bf16[256,512]{1,0:T(8,128)(2,1)} %param.18) | copy-start | bytes 786436
  76.1 33.0 %copy-start.2 = (bf16[256,512]{1,0:T(8,128)(2,1)S(1)}, bf16[256,512]{1,0:T(8,128)(2,1)}, u32[]{:S(2)}) copy-start(bf16[256,512]{1,0:T(8,128)(2,1)} %param.17) | copy-start | bytes 786436
Sparse Core Ops, SparseCore 0:
  108.5 131.8 all-gather.1
